TPU v7x, 256 devices: a whole 4x4x8 slice. The times are simulated.
256 devices in a mesh: batch: 4 (over x_hi, core), hidden: 16 (over x_lo, z), width: 4 (over y).
Axes of the slice: x: 4 (x_hi: 2, x_lo: 2; x = x_hi * 2 + x_lo), y: 4, z: 8, core: 2. Of those that a mesh axis runs over, the one named last changes fastest.
Arguments:
- frames: bfloat16 [4, 512, 1280], P('batch', None, 'hidden'), may hold values from -6 to 6
- adapter_weight: bfloat16 [4, 1280, 16384], P(None, 'hidden', 'width'), may hold values from -0.078125 to 0.078125
- text_embed: bfloat16 [512, 16384], P('batch', 'width'), may hold values from -6 to 6
- audio_len: int32 [4], P('batch'), may hold values from 16 to 64, as said below
- text_len: int32 [4], P('batch'), may hold values from 32 to 112, as said below
- norm_gain: bfloat16 [16384], P('width'), may hold values from 0.5 to 1.5
- gate_up: bfloat16 [16384, 2, 26624], P('width', None, ('batch', 'hidden')), may hold values from -0.046875 to 0.046875
- cotangent: bfloat16 [512, 26624], P('width', ('batch', 'hidden')), may hold values from -0.59765625 to 0.59765625
Outputs:
- hidden: bfloat16 [512, 26624], P('width', ('batch', 'hidden'))
- weight_grad: float32 [4, 1280, 16384], P(None, 'hidden', 'width')
Inputs may be any that keep to these rules, and one draw needn't show every extreme that they name: `audio_len`: some sequence holds exactly 16 audio positions and another exactly 64. audio_len + text_len never exceeds 128, and equals it in some sequence.
All inputs are finite; a program needn't handle non-finite values.
Results may differ from a plain program's by a relative error of at most 0.0059.
Values may be sent and summed in bfloat16 or wider, within the bound.
A program may use at most 64 MiB of HBM per device.

v0:
```python
import jax
import jax.numpy as jnp
from jax import lax
from jax.sharding import PartitionSpec as P

D = 16384
HEAD = 64
norm_eps = 1e-05


def on_device(
    frames, adapter_weight, text_embed, audio_len, text_len, norm_gain, gate_up, cotangent
):
    feat_here = frames.shape[2]
    seq_len = frames.shape[1] // 4
    width_here = adapter_weight.shape[2]
    stacked = frames[0, : 4 * HEAD].reshape(HEAD, 4 * feat_here)
    kernel = adapter_weight.reshape(4 * feat_here, width_here)
    partial_audio = jnp.dot(stacked, kernel, preferred_element_type=jnp.float32)
    audio_part = lax.psum(partial_audio, "hidden")
    positions = jnp.arange(seq_len, dtype=jnp.int32)
    is_audio = positions < audio_len[0]
    is_text = jnp.logical_and(jnp.logical_not(is_audio), positions < audio_len[0] + text_len[0])
    text_vals = jnp.where(is_text[:, None], text_embed.astype(jnp.float32), 0.0)
    stream = jnp.concatenate(
        [jnp.where(is_audio[:HEAD, None], audio_part, text_vals[:HEAD]), text_vals[HEAD:]], axis=0
    )
    gain_vals = norm_gain.astype(jnp.float32)
    sum_squares = lax.psum(jnp.sum(stream * stream, axis=1), "width")
    inv_rms = lax.rsqrt(sum_squares / D + norm_eps)
    normed = (stream * inv_rms[:, None] * gain_vals[None, :]).astype(jnp.bfloat16)
    masked = jnp.where(is_audio[:HEAD, None], stacked, jnp.zeros_like(stacked))
    all_stacked = lax.all_gather(masked, "batch", axis=0, tiled=True)
    all_inv = lax.all_gather(inv_rms[:HEAD], "batch", axis=0, tiled=True)
    all_normed = lax.all_gather(normed, "batch", axis=0, tiled=True)
    weights = gate_up.reshape(width_here, -1)
    half = weights.shape[1] // 2
    partial_pair = jnp.dot(all_normed, weights, preferred_element_type=jnp.float32)
    summed = lax.psum_scatter(partial_pair, "width", scatter_dimension=0, tiled=True)
    gate_vals = summed[:, :half]
    up_vals = summed[:, half:]
    sigmoid_gate = jax.nn.sigmoid(gate_vals)
    silu_gate = gate_vals * sigmoid_gate
    hidden = (silu_gate * up_vals).astype(jnp.bfloat16)
    cot_vals = cotangent[:HEAD].astype(jnp.float32)
    gate_head, up_head, sig_head = (gate_vals[:HEAD], up_vals[:HEAD], sigmoid_gate[:HEAD])
    grad_gate = cot_vals * up_head * sig_head * (1.0 + gate_head * (1.0 - sig_head))
    grad_up = cot_vals * silu_gate[:HEAD]
    inner = jnp.sum(grad_gate * gate_head + grad_up * up_head, axis=1) / D
    grad_pair = jnp.concatenate([grad_gate, grad_up], axis=1).astype(jnp.bfloat16)
    all_pairs = lax.all_gather(grad_pair, "width", axis=0, tiled=True)
    all_inner = lax.all_gather(inner, "width", axis=0, tiled=True)
    partial = lax.dot_general(
        all_pairs, weights, (((1,), (1,)), ((), ())), preferred_element_type=jnp.float32
    )
    head_normed = all_normed.reshape(-1, seq_len, width_here)[:, :HEAD].reshape(-1, width_here)
    head_unit = head_normed.astype(jnp.float32) / gain_vals[None, :]
    share = (gain_vals[None, :] * partial - head_unit * all_inner[:, None]) * all_inv[:, None]
    grad_share = lax.psum_scatter(share, ("batch", "hidden"), scatter_dimension=0, tiled=True)
    audio_grad = lax.all_gather(
        grad_share.astype(jnp.bfloat16), ("batch", "hidden"), axis=0, tiled=True
    )
    weight_grad = lax.dot_general(
        all_stacked, audio_grad, (((0,), (0,)), ((), ())), preferred_element_type=jnp.float32
    )
    return (hidden, weight_grad.reshape(4, feat_here, width_here))


def solution(mesh):
    return jax.shard_map(
        on_device,
        mesh=mesh,
        in_specs=(
            P("batch", None, "hidden"),
            P(None, "hidden", "width"),
            P("batch", "width"),
            P("batch"),
            P("batch"),
            P("width"),
            P("width", None, ("batch", "hidden")),
            P("width", ("batch", "hidden")),
        ),
        out_specs=(P("width", ("batch", "hidden")), P(None, "hidden", "width")),
        check_vma=False,
    )
```

profile of v0, /device:TPU:99, one launch (start us, length us, event | category | flops | bytes accessed | tf_op | source)
XLA Modules:
  0.0 773.7 jit_solution(12971479772562971977)
XLA Ops:
  7.2 0.0 copy-start
  7.2 0.0 copy-start.4
  7.2 0.0 all-reduce.6.cloned.1.call-start
  7.2 0.9 slice.43
  8.2 0.1 copy.11
  8.3 0.1 reshape_squeeze.3
  8.4 0.5 copy-done
  8.9 1.7 fusion.9
  10.6 0.0 all-reduce.6.cloned.1.call-update
  10.6 0.0 all-gather.4.cloned.1.call-start
  12.0 0.0 copy-done.4
  12.0 2.8 convert_select_fusion
  14.8 121.5 %all-reduce.6.cloned.1.call-done = f32[64,4096]{1,0:T(8,128)} async-done(((f32[64,4096]{1,0:T(8,128)}), f32[64,4096]{1,0:T(8,128)}) %all-reduce.6.cloned.1.call-update) | async-done | bytes 1048592 | tf_op jit(solution)/shard_map/psum | solution.py:20
  136.3 2.1 slice_select_fusion
  138.4 0.0 copy-start.1
  138.4 0.0 copy-start.2
  138.4 1.0 copy-done.1
  139.4 0.3 copy-done.2
  139.7 0.2 multiply_reduce_fusion
  139.9 8.8 %psum.15 = f32[128]{0:T(128)S(1)} all-reduce(f32[128]{0:T(128)S(1)} %multiply_reduce_fusion), channel_id=1, replica_groups=mesh['batch'=4,'hidden'=16,'width'=4] {'width'}, use_global_device_ids=true, to_apply=%region_2.3 | all-reduce | flops 128 | bytes 1024 | tf_op jit(solution)/shard_map/psum | solution.py:29
  148.8 2.8 multiply_convert_fusion
  151.6 0.0 all-gather.4.cloned.1.call-update
  151.6 0.0 reduce-scatter.2.cloned.1.call-start
  151.7 51.2 %all-gather.4.cloned.1.call-done = bf16[512,4096]{1,0:T(8,128)(2,1)} async-done(((bf16[128,4096]{1,0:T(8,128)(2,1)}), bf16[512,4096]{1,0:T(8,128)(2,1)}) %all-gather.4.cloned.1.call-update) | async-done | bytes 4194320 | tf_op jit(solution)/shard_map/all_gather | solution.py:35
  202.9 0.0 copy-start.7
  202.9 0.0 copy-start.6
  202.9 0.0 copy-start.5
  202.9 9.1 %fusion.10 = f32[512,832]{0,1:T(8,128)} fusion(bf16[512,4096]{1,0:T(8,128)(2,1)} %all-gather.4.cloned.1.call-done, bf16[4096,832]{0,1:T(8,128)(2,1)} %bitcast.32), kind=kOutput, calls=%fused_computation.30 | convolution fusion | flops 3489660928 | bytes 12713984 | tf_op jit(solution)/shard_map/dot_general | solution.py:38
  212.1 0.0 reduce-scatter.2.cloned.1.call-update
  212.1 0.0 copy-start.3
  212.1 0.0 all-gather.6.cloned.1.call-start
  212.2 0.0 copy-done.7
  212.2 0.6 dynamic-slice
  212.8 0.0 copy-done.6
  212.8 0.6 dynamic-slice.1
  214.7 0.0 copy-done.5
  214.7 0.6 dynamic-slice.2
  215.9 0.1 slice_dynamic-update-slice_fusion
  216.0 6.8 all-reduce.1
  222.8 3.4 slice.63
  226.2 15.0 %reduce-scatter.2.cloned.1.call-done = f32[128,832]{0,1:T(8,128)} async-done(((f32[512,832]{0,1:T(8,128)}), f32[128,832]{0,1:T(8,128)}) %reduce-scatter.2.cloned.1.call-update) | async-done | bytes 426000 | tf_op jit(solution)/shard_map/reduce_scatter | solution.py:39
  241.2 1.7 add_divide_fusion
  242.9 0.0 copy-done.3
  242.9 1.2 add_reduce_fusion
  244.2 0.1 copy.12
  244.3 9.8 %all_gather.20 = bf16[256,832]{1,0:T(8,128)(2,1)S(1)} all-gather(bf16[64,832]{1,0:T(8,128)(2,1)S(1)} %copy.12), channel_id=1, replica_groups=mesh['batch'=4,'hidden'=16,'width'=4] {'width'}, dimensions={0}, use_global_device_ids=true | all-gather | bytes 532480 | tf_op jit(solution)/shard_map/all_gather | solution.py:51
  254.1 0.1 multiply_dynamic-update-slice_fusion
  254.2 7.6 all-reduce
  261.7 8.1 %fusion.1 = f32[256,4096]{1,0:T(8,128)} fusion(bf16[256,832]{1,0:T(8,128)(2,1)S(1)} %all_gather.20, bf16[4096,832]{0,1:T(8,128)(2,1)} %bitcast.33, bf16[256,4096]{1,0:T(8,128)(2,1)} %bitcast.28, f32[256]{0:T(256)S(1)} %all-reduce.1, f32[256]{0:T(256)S(1)} %all-reduce, f32[4096]{0:T(1024)S(1)} %convert_element_type.26), kind=kOutput, calls=%fused_computation.2 | convolution fusion | flops 1751121920 | bytes 13551616 | tf_op jit(solution)/shard_map/dot_general | solution.py:53
  269.8 281.6 %all-reduce.7 = bf16[256,4096]{1,0:T(8,128)(2,1)} all-reduce(f32[256,4096]{1,0:T(8,128)} %fusion.1), channel_id=3, replica_groups=mesh['batch'=4,'hidden'=16,'width'=4] {'batch','hidden'}, use_global_device_ids=true, to_apply=%region_5.6.clone | all-reduce | flops 1048576 | bytes 6291456
  551.4 1.5 fusion.7
  552.9 0.0 all-gather.6.cloned.1.call-update
  552.9 0.1 broadcast_select_fusion
  553.0 17.8 %all_gather.19 = bf16[256,320]{1,0:T(8,128)(2,1)S(1)} all-gather(bf16[64,320]{1,0:T(8,128)(2,1)S(1)} %broadcast_select_fusion), channel_id=1, replica_groups=mesh['batch'=4,'hidden'=16,'width'=4] {'batch'}, dimensions={0}, use_global_device_ids=true | all-gather | bytes 204800 | tf_op jit(solution)/shard_map/all_gather | solution.py:33
  570.8 187.6 %all-gather.6.cloned.1.call-done = bf16[64,4,4096]{2,1,0:T(4,128)(2,1)} async-done(((bf16[1,4,4096]{2,1,0:T(4,128)(2,1)}), bf16[64,4,4096]{2,1,0:T(4,128)(2,1)}) %all-gather.6.cloned.1.call-update) | async-done | bytes 2097168 | tf_op jit(solution)/shard_map/all_gather | solution.py:60
  758.4 4.0 reshape.44
  762.4 4.8 fusion.11
  (7 shorter events, 0.1 us)
Async XLA Ops:
  7.2 1.8 copy-start
  7.2 4.8 copy-start.4
  7.2 129.1 %all-reduce.6.cloned.1.call-start = ((), (), s32[]{:S(2)}) async-start(), calls=%async_computation.1 | async-start | bytes 2097152 | tf_op jit(solution)/shard_map/psum | solution.py:20
  10.6 192.3 %all-gather.4.cloned.1.call-start = ((), (), s32[]{:S(2)}) async-start(), calls=%async_computation.2 | async-start | bytes 5242880 | tf_op jit(solution)/shard_map/all_gather | solution.py:35
  138.4 1.0 copy-start.1
  138.4 1.3 copy-start.2
  151.6 89.6 %reduce-scatter.2.cloned.1.call-start = ((), (), s32[]{:S(2)}) async-start(), calls=%async_computation.3 | async-start | bytes 2129920 | tf_op jit(solution)/shard_map/reduce_scatter | solution.py:39
  202.9 9.2 %copy-start.7 = (u32[256]{0:T(256)S(1)}, u32[256]{0:T(256)}, u32[]{:S(2)}) copy-start(u32[256]{0:T(256)} %constant.21) | copy-start | bytes 3076
  202.9 9.9 %copy-start.6 = (u32[256]{0:T(256)S(1)}, u32[256]{0:T(256)}, u32[]{:S(2)}) copy-start(u32[256]{0:T(256)} %constant.26) | copy-start | bytes 3076
  202.9 11.8 %copy-start.5 = (u32[256]{0:T(256)S(1)}, u32[256]{0:T(256)}, u32[]{:S(2)}) copy-start(u32[256]{0:T(256)} %constant.33) | copy-start | bytes 3076
  212.1 30.9 %copy-start.3 = (bf16[128,416]{0,1:T(8,128)(2,1)S(1)}, bf16[128,416]{0,1:T(8,128)(2,1)}, u32[]{:S(2)}) copy-start(bf16[128,416]{0,1:T(8,128)(2,1)} %param.15) | copy-start | bytes 319492
  212.1 546.3 %all-gather.6.cloned.1.call-start = ((), (), s32[]{:S(2)}) async-start(), calls=%async_computation.4 | async-start | bytes 2129920 | tf_op jit(solution)/shard_map/all_gather | solution.py:60
Sparse Core Ops, SparseCore 0:
  10.8 125.5 all-reduce.5
  151.7 51.1 all-gather.3
  212.2 28.9 reduce-scatter.1
  553.1 205.2 all-gather.5
where the time goes:
time: 774 us
  waiting for transfers between devices  375 us (48%)
  blocking collectives  332 us (43%)
  matrix products  23.7 us (3%)
  between operations  17.1 us (2%)
  local copies, waits for them, and re-layouts  13.9 us (2%)
  other arithmetic  11.1 us (1%)
    unnamed x3, blocking collectives  296 us
    all_gather x1, waiting for transfers between devices, on_device(): lax.all_gather(grad_share.astype(jnp.bfloat16), ('batch', 'hidden'), axis...  188 us
    psum x1, waiting for transfers between devices, on_device(): audio_part = lax.psum(partial_audio, 'hidden')  121 us
    all_gather x1, waiting for transfers between devices, on_device(): all_normed = lax.all_gather(normed, 'batch', axis=0, tiled=True)  51.2 us
    all_gather x1, blocking collectives, on_device(): all_stacked = lax.all_gather(masked, 'batch', axis=0, tiled=True)  17.8 us
  transfers between devices with their start and end apart: 4, of which 4 were waited for; matrix products, arithmetic and copies ran while one was open for 1% of the time, Pallas kernels for 0%

commit v1 on v0

--- a/solution.py
+++ b/solution.py
@@ -57,8 +57,14 @@
     head_unit = head_normed.astype(jnp.float32) / gain_vals[None, :]
     share = (gain_vals[None, :] * partial - head_unit * all_inner[:, None]) * all_inv[:, None]
     grad_share = lax.psum_scatter(share, ("batch", "hidden"), scatter_dimension=0, tiled=True)
-    audio_grad = lax.all_gather(
-        grad_share.astype(jnp.bfloat16), ("batch", "hidden"), axis=0, tiled=True
+    audio_grad = jnp.concatenate(
+        lax.all_to_all(
+            jnp.stack(lax.axis_size(("batch", "hidden")) * [grad_share.astype(jnp.bfloat16)]),
+            axis_name=("batch", "hidden"),
+            split_axis=0,
+            concat_axis=0,
+        ),
+        axis=0,
     )
     weight_grad = lax.dot_general(
         all_stacked, audio_grad, (((0,), (0,)), ((), ())), preferred_element_type=jnp.float32

time: 774 us -> 654 us (0.84)
  waiting for transfers between devices: 375 us -> 224 us
  starting transfers between devices: 0.16 us -> 29.6 us
    all_gather x1 -> x0, waiting for transfers between devices: 188 us -> none  [on_device(): lax.all_gather(grad_share.astype(jnp.bfloat16), ('batch', 'hidden'), axis...]
    all_to_all x0 -> x1, waiting for transfers between devices: none -> 36.1 us  [on_device(): lax.all_to_all(jnp.stack(lax.axis_size(('batch', 'hidden')) * [grad_share...]
    all_to_all x0 -> x1, starting transfers between devices: none -> 29.5 us  [on_device(): lax.all_to_all(jnp.stack(lax.axis_size(('batch', 'hidden')) * [grad_share...]
where the time goes in v1:
time: 654 us; the launch traced here: 649 us
  blocking collectives  328 us (50%)
  waiting for transfers between devices  224 us (34%)
  starting transfers between devices  29.6 us (5%)
  matrix products  23.7 us (4%)
  between operations  17.1 us (3%)
  local copies, waits for them, and re-layouts  15.7 us (2%)
  other arithmetic  11.1 us (2%)
    unnamed x3, blocking collectives  296 us
    psum x1, waiting for transfers between devices, on_device(): audio_part = lax.psum(partial_audio, 'hidden')  121 us
    all_gather x1, waiting for transfers between devices, on_device(): all_normed = lax.all_gather(normed, 'batch', axis=0, tiled=True)  51.2 us
    all_to_all x1, waiting for transfers between devices, on_device(): lax.all_to_all(jnp.stack(lax.axis_size(('batch', 'hidden')) * [grad_share...  36.1 us
    all_to_all x1, starting transfers between devices, on_device(): lax.all_to_all(jnp.stack(lax.axis_size(('batch', 'hidden')) * [grad_share...  29.5 us
    reduce_scatter x1, waiting for transfers between devices, on_device(): lax.psum_scatter(partial_pair, 'width', scatter_dimension=0, tiled=True)  15.1 us
  transfers between devices with their start and end apart: 4, of which 4 were waited for; matrix products, arithmetic and copies ran while one was open for 1% of the time, Pallas kernels for 0%

profile of v1, /device:TPU:99, one launch (start us, length us, event | category | flops | bytes accessed | tf_op | source)
XLA Modules:
  0.0 648.8 jit_solution(13225152780866141676)
XLA Ops:
  7.2 0.0 copy-start
  7.2 0.0 copy-start.4
  7.2 0.0 all-reduce.6.cloned.1.call-start
  7.2 0.9 slice.43
  8.2 0.1 copy.12
  8.3 0.1 reshape_squeeze.3
  8.4 0.5 copy-done
  8.9 1.7 fusion.8
  10.6 0.0 all-reduce.6.cloned.1.call-update
  10.6 0.0 all-gather.2.cloned.1.call-start
  12.0 0.0 copy-done.4
  12.0 2.8 convert_select_fusion
  14.8 121.5 %all-reduce.6.cloned.1.call-done = f32[64,4096]{1,0:T(8,128)} async-done(((f32[64,4096]{1,0:T(8,128)}), f32[64,4096]{1,0:T(8,128)}) %all-reduce.6.cloned.1.call-update) | async-done | bytes 1048592 | tf_op jit(solution)/shard_map/psum | solution.py:20
  136.3 2.1 slice_select_fusion
  138.4 0.0 copy-start.1
  138.4 0.0 copy-start.2
  138.4 1.0 copy-done.1
  139.4 0.3 copy-done.2
  139.7 0.2 multiply_reduce_fusion
  139.9 8.8 %psum.15 = f32[128]{0:T(128)S(1)} all-reduce(f32[128]{0:T(128)S(1)} %multiply_reduce_fusion), channel_id=1, replica_groups=mesh['batch'=4,'hidden'=16,'width'=4] {'width'}, use_global_device_ids=true, to_apply=%region_2.3 | all-reduce | flops 128 | bytes 1024 | tf_op jit(solution)/shard_map/psum | solution.py:29
  148.8 2.8 multiply_convert_fusion
  151.6 0.0 all-gather.2.cloned.1.call-update
  151.6 0.0 reduce-scatter.2.cloned.1.call-start
  151.7 51.2 %all-gather.2.cloned.1.call-done = bf16[512,4096]{1,0:T(8,128)(2,1)} async-done(((bf16[128,4096]{1,0:T(8,128)(2,1)}), bf16[512,4096]{1,0:T(8,128)(2,1)}) %all-gather.2.cloned.1.call-update) | async-done | bytes 4194320 | tf_op jit(solution)/shard_map/all_gather | solution.py:35
  202.9 0.0 copy-start.7
  202.9 0.0 copy-start.6
  202.9 0.0 copy-start.5
  202.9 9.1 %fusion.9 = f32[512,832]{0,1:T(8,128)} fusion(bf16[512,4096]{1,0:T(8,128)(2,1)} %all-gather.2.cloned.1.call-done, bf16[4096,832]{0,1:T(8,128)(2,1)} %bitcast.32), kind=kOutput, calls=%fused_computation.29 | convolution fusion | flops 3489660928 | bytes 12713984 | tf_op jit(solution)/shard_map/dot_general | solution.py:38
  212.1 0.0 reduce-scatter.2.cloned.1.call-update
  212.1 0.0 copy-start.3
  212.1 0.0 copy-done.7
  212.1 0.6 dynamic-slice
  212.7 0.0 copy-done.6
  212.7 0.6 dynamic-slice.1
  214.6 0.0 copy-done.5
  214.6 0.6 dynamic-slice.2
  215.9 0.1 slice_dynamic-update-slice_fusion
  216.0 6.8 %all-reduce.1 = f32[256]{0:T(256)S(1)} all-reduce(f32[256]{0:T(256)S(1)} %slice_dynamic-update-slice_fusion), channel_id=1, replica_groups=mesh['batch'=4,'hidden'=16,'width'=4] {'batch'}, use_global_device_ids=true, to_apply=%add.1 | all-reduce | flops 256 | bytes 2048
  222.7 3.4 slice.63
  226.1 15.1 %reduce-scatter.2.cloned.1.call-done = f32[128,832]{0,1:T(8,128)} async-done(((f32[512,832]{0,1:T(8,128)}), f32[128,832]{0,1:T(8,128)}) %reduce-scatter.2.cloned.1.call-update) | async-done | bytes 426000 | tf_op jit(solution)/shard_map/reduce_scatter | solution.py:39
  241.2 1.7 add_divide_fusion
  242.9 0.0 copy-done.3
  242.9 1.2 add_reduce_fusion
  244.2 0.1 copy.14
  244.3 9.8 %all_gather.17 = bf16[256,832]{1,0:T(8,128)(2,1)S(1)} all-gather(bf16[64,832]{1,0:T(8,128)(2,1)S(1)} %copy.14), channel_id=1, replica_groups=mesh['batch'=4,'hidden'=16,'width'=4] {'width'}, dimensions={0}, use_global_device_ids=true | all-gather | bytes 532480 | tf_op jit(solution)/shard_map/all_gather | solution.py:51
  254.1 0.1 multiply_dynamic-update-slice_fusion
  254.2 7.6 %all-reduce = f32[256]{0:T(256)S(1)} all-reduce(f32[256]{0:T(256)S(1)} %multiply_dynamic-update-slice_fusion), channel_id=1, replica_groups=mesh['batch'=4,'hidden'=16,'width'=4] {'width'}, use_global_device_ids=true, to_apply=%add | all-reduce | flops 256 | bytes 2048
  261.7 8.1 %fusion.1 = f32[256,4096]{1,0:T(8,128)} fusion(bf16[256,832]{1,0:T(8,128)(2,1)S(1)} %all_gather.17, bf16[4096,832]{0,1:T(8,128)(2,1)} %bitcast.33, bf16[256,4096]{1,0:T(8,128)(2,1)} %bitcast.26, f32[256]{0:T(256)S(1)} %all-reduce.1, f32[256]{0:T(256)S(1)} %all-reduce, f32[4096]{0:T(1024)S(1)} %convert_element_type.26), kind=kOutput, calls=%fused_computation.2 | convolution fusion | flops 1751121920 | bytes 13551616 | tf_op jit(solution)/shard_map/dot_general | solution.py:53
  269.8 281.6 %all-reduce.7 = bf16[256,4096]{1,0:T(8,128)(2,1)} all-reduce(f32[256,4096]{1,0:T(8,128)} %fusion.1), channel_id=3, replica_groups=mesh['batch'=4,'hidden'=16,'width'=4] {'batch','hidden'}, use_global_device_ids=true, to_apply=%region_5.6.clone | all-reduce | flops 1048576 | bytes 6291456
  551.4 0.9 dynamic-slice_convert_fusion
  552.3 2.3 stack.2
  554.6 29.5 %all-to-all-start = ((bf16[64,4,4096]{2,1,0:T(4,128)(2,1)}), bf16[64,4,4096]{2,1,0:T(4,128)(2,1)}, u32[]{:S(2)}, u32[]{:S(2)}) async-start(bf16[64,4,4096]{2,1,0:T(4,128)(2,1)} %stack.2), calls=%async_computation.1 | async-start | bytes 4194304 | tf_op jit(solution)/shard_map/all_to_all | solution.py:61
  584.1 0.1 broadcast_select_fusion
  584.2 13.0 %all_gather.16 = bf16[256,320]{1,0:T(8,128)(2,1)S(1)} all-gather(bf16[64,320]{1,0:T(8,128)(2,1)S(1)} %broadcast_select_fusion), channel_id=1, replica_groups=mesh['batch'=4,'hidden'=16,'width'=4] {'batch'}, dimensions={0}, use_global_device_ids=true | all-gather | bytes 204800 | tf_op jit(solution)/shard_map/all_gather | solution.py:33
  597.3 0.1 copy.13
  597.4 36.1 %all-to-all-done = bf16[64,4,4096]{2,1,0:T(4,128)(2,1)} async-done(((bf16[64,4,4096]{2,1,0:T(4,128)(2,1)}), bf16[64,4,4096]{2,1,0:T(4,128)(2,1)}, u32[]{:S(2)}, u32[]{:S(2)}) %all-to-all-start) | async-done | bytes 2097184 | tf_op jit(solution)/shard_map/all_to_all | solution.py:61
  633.5 4.0 reshape.51
  637.5 4.8 fusion.10
  (7 shorter events, 0.1 us)
Async XLA Ops:
  7.2 1.8 copy-start
  7.2 4.8 copy-start.4
  7.2 129.1 %all-reduce.6.cloned.1.call-start = ((), (), s32[]{:S(2)}) async-start(), calls=%async_computation.2 | async-start | bytes 2097152 | tf_op jit(solution)/shard_map/psum | solution.py:20
  10.6 192.3 %all-gather.2.cloned.1.call-start = ((), (), s32[]{:S(2)}) async-start(), calls=%async_computation.3 | async-start | bytes 5242880 | tf_op jit(solution)/shard_map/all_gather | solution.py:35
  138.4 1.0 copy-start.1
  138.4 1.3 copy-start.2
  151.6 89.6 %reduce-scatter.2.cloned.1.call-start = ((), (), s32[]{:S(2)}) async-start(), calls=%async_computation.4 | async-start | bytes 2129920 | tf_op jit(solution)/shard_map/reduce_scatter | solution.py:39
  202.9 9.2 %copy-start.7 = (u32[256]{0:T(256)S(1)}, u32[256]{0:T(256)}, u32[]{:S(2)}) copy-start(u32[256]{0:T(256)} %constant.21) | copy-start | bytes 3076
  202.9 9.8 %copy-start.6 = (u32[256]{0:T(256)S(1)}, u32[256]{0:T(256)}, u32[]{:S(2)}) copy-start(u32[256]{0:T(256)} %constant.26) | copy-start | bytes 3076
  202.9 11.7 %copy-start.5 = (u32[256]{0:T(256)S(1)}, u32[256]{0:T(256)}, u32[]{:S(2)}) copy-start(u32[256]{0:T(256)} %constant.33) | copy-start | bytes 3076
  212.1 30.9 %copy-start.3 = (bf16[128,416]{0,1:T(8,128)(2,1)S(1)}, bf16[128,416]{0,1:T(8,128)(2,1)}, u32[]{:S(2)}) copy-start(bf16[128,416]{0,1:T(8,128)(2,1)} %param.15) | copy-start | bytes 319492
  554.6 78.9 %all-to-all-start = ((bf16[64,4,4096]{2,1,0:T(4,128)(2,1)}), bf16[64,4,4096]{2,1,0:T(4,128)(2,1)}, u32[]{:S(2)}, u32[]{:S(2)}) async-start(bf16[64,4,4096]{2,1,0:T(4,128)(2,1)} %stack.2), calls=%async_computation.1 | async-start | bytes 4194304 | tf_op jit(solution)/shard_map/all_to_all | solution.py:61
Sparse Core Ops, SparseCore 0:
  10.8 125.5 all-reduce.5
  151.7 51.1 all-gather.1
  212.2 28.9 reduce-scatter.1
